TPU v7x, 32 devices: a whole 2x2x4 slice. The times are simulated.
32 devices in a mesh: seq: 8 (over z, core), head: 4 (over y, x).
Axes of the slice: x: 2, y: 2, z: 4, core: 2. Of those that a mesh axis runs over, the one named last changes fastest.
Arguments:
- video_query: bfloat16 [4096, 3072], P(('seq', 'head')), may hold values from -8 to 8
- video_key: bfloat16 [4096, 3072], P(('seq', 'head')), may hold values from -8 to 8
- video_value: bfloat16 [4096, 3072], P(('seq', 'head')), may hold values from -6 to 6
- video_grad: bfloat16 [4096, 3072], P(('seq', 'head')), may hold values from -6 to 6
- text_query: bfloat16 [256, 3072], P(None, 'head'), may hold values from -8 to 8
- text_key: bfloat16 [256, 3072], P(None, 'head'), may hold values from -8 to 8
- text_value: bfloat16 [256, 3072], P(None, 'head'), may hold values from -6 to 6
- text_grad: bfloat16 [256, 3072], P(None, 'head'), may hold values from -6 to 6
- tile_list: int32 [32, 8], replicated, may hold values from 0 to 31, as said below
- tile_count: int32 [32], replicated, may hold values from 1 to 8, as said below
- text_mask: int32 [256], replicated, may hold values from 0 to 1, as said below
Outputs:
- attended_video: bfloat16 [4096, 3072], P(('seq', 'head'))
- video_query_grad: bfloat16 [4096, 3072], P(('seq', 'head'))
- video_key_grad: bfloat16 [4096, 3072], P(('seq', 'head'))
- video_value_grad: bfloat16 [4096, 3072], P(('seq', 'head'))
- attended_text: bfloat16 [256, 3072], P(None, 'head')
- text_query_grad: bfloat16 [256, 3072], P(None, 'head')
- text_key_grad: bfloat16 [256, 3072], P(None, 'head')
- text_value_grad: bfloat16 [256, 3072], P(None, 'head')
Inputs may be any that keep to these rules, and one draw needn't show every extreme that they name: `tile_list`: the 8 entries of one query tile's list are distinct. Query tiles fall in aligned blocks of 4; the used entries of one block together name at most 2 distinct tiles of any other block of 4 tiles, and every block names exactly 2 from some other block. `tile_count`: every aligned block of 4 query tiles has a tile that uses all 8 entries. `text_mask`: the ones form a prefix of at least 64 entries.
All inputs are finite; a program needn't handle non-finite values.
Results may differ from a plain program's by a relative error of at most 0.012.
Values may be sent and summed in bfloat16 or wider, within the bound.
A program may use at most 192 MiB of HBM per device.

v0:
```python
import jax
import jax.numpy as jnp
from jax import lax
from jax.sharding import PartitionSpec as P

HD = 128
TXT = 256
TILE = 128
KT = 8
MOST = 2
NEGATIVE = -1e30
HIGHEST_PRECISION = lax.Precision.HIGHEST


def split_product(form, weights, data):
    upper = weights.astype(jnp.bfloat16)
    lower = (weights - upper.astype(jnp.float32)).astype(jnp.bfloat16)
    return jnp.einsum(form, upper, data, preferred_element_type=jnp.float32) + jnp.einsum(
        form, lower, data, preferred_element_type=jnp.float32
    )


def block_scores(query_blk, key_blk, live_blk, factor):
    scores = (
        jnp.einsum("bthd,bkhd->bhtk", query_blk, key_blk, preferred_element_type=jnp.float32)
        * factor
    )
    scores = jnp.where(live_blk[:, None, None, :], scores, NEGATIVE)
    maximum = jnp.max(scores, axis=-1)
    log_total = maximum + jnp.log(jnp.sum(jnp.exp(scores - maximum[..., None]), axis=-1))
    return (scores, log_total)


def block_forward(scores, log_total, value_blk, grad_blk):
    weights = jnp.exp(scores - log_total[..., None]).astype(jnp.bfloat16)
    output = jnp.einsum("bhtk,bkhd->bthd", weights, value_blk, preferred_element_type=jnp.float32)
    offset = jnp.sum(grad_blk.astype(jnp.float32) * output, axis=-1)
    return (output, jnp.transpose(offset, (0, 2, 1)))


def block_backward(scores, log_total, offset, query_blk, key_blk, value_blk, grad_blk, factor):
    probability = jnp.exp(scores - log_total[..., None])
    weights = probability.astype(jnp.bfloat16)
    prob_grad = jnp.einsum(
        "bthd,bkhd->bhtk", grad_blk, value_blk, preferred_element_type=jnp.float32
    )
    score_grad = (probability * (prob_grad - offset[..., None])).astype(jnp.bfloat16)
    query_grad = (
        jnp.einsum("bhtk,bkhd->bthd", score_grad, key_blk, preferred_element_type=jnp.float32)
        * factor
    )
    key_grad = (
        jnp.einsum("bhtk,bthd->bkhd", score_grad, query_blk, preferred_element_type=jnp.float32)
        * factor
    )
    value_grad = jnp.einsum(
        "bhtk,bthd->bkhd", weights, grad_blk, preferred_element_type=jnp.float32
    )
    return (query_grad, key_grad, value_grad)


def spread_grads(pool_total, text_total, grad_blk, pool_slot):
    block_tiles = grad_blk.shape[0]
    tile_part = grad_blk[:, : KT * TILE].reshape(block_tiles, KT, TILE, pool_total.shape[2])
    return (
        pool_total.at[pool_slot].add(tile_part),
        text_total + jnp.sum(grad_blk[:, KT * TILE :], axis=0),
    )


def body(
    video_query,
    video_key,
    video_value,
    video_grad,
    text_query,
    text_key,
    text_value,
    text_grad,
    tile_list,
    tile_count,
    text_mask,
):
    factor = HD ** (-0.5)
    groups = lax.axis_size("seq")
    own_group = lax.axis_index("seq")
    query_rows, key_rows, value_rows, grad_rows = (
        lax.all_to_all(video_query, "head", split_axis=1, concat_axis=0, tiled=True),
        lax.all_to_all(video_key, "head", split_axis=1, concat_axis=0, tiled=True),
        lax.all_to_all(video_value, "head", split_axis=1, concat_axis=0, tiled=True),
        lax.all_to_all(video_grad, "head", split_axis=1, concat_axis=0, tiled=True),
    )
    token_rows, feature_width = query_rows.shape
    head_count = feature_width // HD
    shard_tiles = token_rows // TILE
    tile_total = tile_list.shape[0]
    text_ok = text_mask > 0
    entry_live = jnp.arange(KT)[None, :] < tile_count[:, None]
    tile_hits = (tile_list[:, :, None] == jnp.arange(tile_total)[None, None, :]) & entry_live[
        :, :, None
    ]
    wanted = jnp.any(
        jnp.any(tile_hits, axis=1).reshape(groups, shard_tiles, tile_total), axis=1
    ).reshape(groups, groups, shard_tiles)
    slot_rank = jnp.cumsum(wanted.astype(jnp.int32), axis=2) - 1
    distinct = (jnp.arange(groups)[:, None] != jnp.arange(groups)[None, :])[:, :, None, None]
    select = (
        wanted[:, :, None, :]
        & (slot_rank[:, :, None, :] == jnp.arange(MOST)[None, None, :, None])
        & distinct
    )
    outgoing = lax.dynamic_index_in_dim(select, own_group, 1, keepdims=False)
    incoming = lax.dynamic_index_in_dim(select, own_group, 0, keepdims=False)
    picker = outgoing.reshape(groups * MOST, shard_tiles).astype(jnp.bfloat16)
    send_keys = jnp.dot(
        picker,
        key_rows.reshape(shard_tiles, TILE * feature_width),
        preferred_element_type=jnp.float32,
    )
    send_keys = send_keys.astype(jnp.bfloat16).reshape(groups, MOST * TILE, feature_width)
    send_values = jnp.dot(
        picker,
        value_rows.reshape(shard_tiles, TILE * feature_width),
        preferred_element_type=jnp.float32,
    )
    send_values = send_values.astype(jnp.bfloat16).reshape(groups, MOST * TILE, feature_width)
    owner_base = (
        jnp.arange(groups, dtype=jnp.int32)[:, None, None] * shard_tiles
        + jnp.arange(shard_tiles, dtype=jnp.int32)[None, None, :]
    )
    slot_ids = jnp.where(
        jnp.any(incoming, axis=2), jnp.sum(jnp.where(incoming, owner_base, 0), axis=2), -1
    ).reshape(groups * MOST)
    pool_ids = jnp.concatenate(
        [own_group * shard_tiles + jnp.arange(shard_tiles, dtype=jnp.int32), slot_ids]
    )
    pool_size = shard_tiles + groups * MOST
    my_list = lax.dynamic_slice_in_dim(tile_list, own_group * shard_tiles, shard_tiles, 0)
    my_count = lax.dynamic_slice_in_dim(tile_count, own_group * shard_tiles, shard_tiles, 0)
    pool_match = my_list[:, :, None] == pool_ids[None, None, :]
    pool_slot = jnp.sum(jnp.where(pool_match, jnp.arange(pool_size, dtype=jnp.int32), 0), axis=2)
    live_entry = jnp.any(pool_match, axis=2) & (jnp.arange(KT)[None, :] < my_count[:, None])
    text_query3 = text_query.reshape(TXT, head_count, HD)
    text_key3 = text_key.reshape(TXT, head_count, HD)
    text_value3 = text_value.reshape(TXT, head_count, HD)
    text_grad3 = text_grad.reshape(TXT, head_count, HD)
    block_tiles = min(shard_tiles, max(1, 512 // TILE))
    block_count = shard_tiles // block_tiles
    query_blocks = query_rows.reshape(block_count, block_tiles, TILE, head_count, HD)
    grad_blocks = grad_rows.reshape(block_count, block_tiles, TILE, head_count, HD)
    slot_blocks = pool_slot.reshape(block_count, block_tiles, KT)
    live_blocks = jnp.concatenate(
        [
            jnp.repeat(live_entry, TILE, axis=1),
            jnp.broadcast_to(text_ok[None, :], (shard_tiles, TXT)),
        ],
        axis=1,
    )
    live_blocks = live_blocks.reshape(block_count, block_tiles, KT * TILE + TXT)
    local_keys = key_rows.reshape(shard_tiles, TILE, feature_width)
    local_values = value_rows.reshape(shard_tiles, TILE, feature_width)

    def build_pool(received):
        got_keys, got_values = received
        return (
            jnp.concatenate(
                [local_keys, got_keys.reshape(groups * MOST, TILE, feature_width)], axis=0
            ),
            jnp.concatenate(
                [local_values, got_values.reshape(groups * MOST, TILE, feature_width)], axis=0
            ),
        )

    def block_rows(pool, slot_blk, text_part):
        picked = pool[slot_blk].reshape(block_tiles, KT * TILE, head_count, HD)
        return jnp.concatenate(
            [picked, jnp.broadcast_to(text_part[None], (block_tiles, TXT, head_count, HD))], axis=1
        )

    pool_keys, pool_values = build_pool(
        (
            lax.all_to_all(send_keys, "seq", split_axis=0, concat_axis=0, tiled=True),
            lax.all_to_all(send_values, "seq", split_axis=0, concat_axis=0, tiled=True),
        )
    )
    start = (
        jnp.zeros((pool_size, TILE, feature_width), jnp.float32),
        jnp.zeros((pool_size, TILE, feature_width), jnp.float32),
        jnp.zeros((TXT, head_count, HD), jnp.float32),
        jnp.zeros((TXT, head_count, HD), jnp.float32),
    )

    def forward_step(running, inputs):
        query_blk, grad_blk, slot_blk, live_blk = inputs
        key_blk = block_rows(pool_keys, slot_blk, text_key3)
        value_blk = block_rows(pool_values, slot_blk, text_value3)
        scores, log_total = block_scores(query_blk, key_blk, live_blk, factor)
        output, offset = block_forward(scores, log_total, value_blk, grad_blk)
        return (running, (output.astype(jnp.bfloat16), log_total, offset))

    unused, forwards = lax.scan(
        forward_step, None, (query_blocks, grad_blocks, slot_blocks, live_blocks)
    )
    attended_blocks, total_blocks, offset_blocks = forwards
    again_keys, again_values = build_pool(
        (
            lax.all_to_all(send_keys, "seq", split_axis=0, concat_axis=0, tiled=True),
            lax.all_to_all(send_values, "seq", split_axis=0, concat_axis=0, tiled=True),
        )
    )

    def backward_step(running, inputs):
        key_acc, value_acc, text_key_acc, text_value_acc = running
        query_blk, grad_blk, slot_blk, live_blk, log_total, offset = inputs
        key_blk = block_rows(again_keys, slot_blk, text_key3)
        value_blk = block_rows(again_values, slot_blk, text_value3)
        scores, unused_total = block_scores(query_blk, key_blk, live_blk, factor)
        query_grad, key_grad, value_grad = block_backward(
            scores, log_total, offset, query_blk, key_blk, value_blk, grad_blk, factor
        )
        key_acc, text_key_acc = spread_grads(key_acc, text_key_acc, key_grad, slot_blk)
        value_acc, text_value_acc = spread_grads(value_acc, text_value_acc, value_grad, slot_blk)
        return ((key_acc, value_acc, text_key_acc, text_value_acc), query_grad.astype(jnp.bfloat16))

    finals, query_grad_blocks = lax.scan(
        backward_step,
        start,
        (query_blocks, grad_blocks, slot_blocks, live_blocks, total_blocks, offset_blocks),
    )
    key_acc, value_acc, text_key_acc, text_value_acc = finals
    back_keys, back_values = (
        lax.all_to_all(
            key_acc[shard_tiles:].reshape(groups, MOST * TILE, feature_width),
            "seq",
            split_axis=0,
            concat_axis=0,
            tiled=True,
        ),
        lax.all_to_all(
            value_acc[shard_tiles:].reshape(groups, MOST * TILE, feature_width),
            "seq",
            split_axis=0,
            concat_axis=0,
            tiled=True,
        ),
    )
    out_flat = outgoing.reshape(groups * MOST, shard_tiles)
    target_tile = jnp.where(
        jnp.any(out_flat, axis=1),
        jnp.sum(jnp.where(out_flat, jnp.arange(shard_tiles, dtype=jnp.int32)[None, :], 0), axis=1),
        shard_tiles,
    )
    own_key_grad = (
        key_acc[:shard_tiles]
        .at[target_tile]
        .add(back_keys.reshape(groups * MOST, TILE, feature_width), mode="drop")
    )
    own_value_grad = (
        value_acc[:shard_tiles]
        .at[target_tile]
        .add(back_values.reshape(groups * MOST, TILE, feature_width), mode="drop")
    )
    key_rows3 = key_rows.reshape(token_rows, head_count, HD)
    value_rows3 = value_rows.reshape(token_rows, head_count, HD)
    text_query32 = text_query3.astype(jnp.float32)
    text_key32 = text_key3.astype(jnp.float32)
    text_value32 = text_value3.astype(jnp.float32)
    text_grad32 = text_grad3.astype(jnp.float32)
    video_scores = (
        jnp.einsum("thd,khd->htk", text_query3, key_rows3, preferred_element_type=jnp.float32)
        * factor
    )
    text_scores = (
        jnp.einsum("thd,khd->htk", text_query3, text_key3, preferred_element_type=jnp.float32)
        * factor
    )
    text_scores = jnp.where(text_ok[None, None, :], text_scores, NEGATIVE)
    maximum = jnp.maximum(
        lax.pmax(jnp.max(video_scores, axis=-1), "seq"), jnp.max(text_scores, axis=-1)
    )
    video_exp = jnp.exp(video_scores - maximum[..., None])
    denominator, numerator = lax.psum(
        (jnp.sum(video_exp, axis=-1), split_product("htk,khd->thd", video_exp, value_rows3)), "seq"
    )
    text_exp = jnp.exp(text_scores - maximum[..., None])
    denominator = denominator + jnp.sum(text_exp, axis=-1)
    numerator = numerator + jnp.einsum(
        "htk,khd->thd", text_exp, text_value32, precision=HIGHEST_PRECISION
    )
    log_total = maximum + jnp.log(denominator)
    text_out = numerator / denominator.T[:, :, None]
    video_prob = jnp.exp(video_scores - log_total[..., None])
    text_prob = jnp.exp(text_scores - log_total[..., None])
    text_offset = jnp.sum(text_grad32 * text_out, axis=-1).T
    video_dscore = video_prob * (
        jnp.einsum("thd,khd->htk", text_grad3, value_rows3, preferred_element_type=jnp.float32)
        - text_offset[..., None]
    )
    text_dscore = text_prob * (
        jnp.einsum("thd,khd->htk", text_grad3, text_value3, preferred_element_type=jnp.float32)
        - text_offset[..., None]
    )
    query_part = split_product("htk,khd->thd", video_dscore, key_rows3) * factor
    video_key_from_text = split_product("htk,thd->khd", video_dscore, text_query3) * factor
    video_value_from_text = split_product("htk,thd->khd", video_prob, text_grad3)
    query_sum, key_sum, value_sum = lax.psum((query_part, text_key_acc, text_value_acc), "seq")
    text_query_grad = (
        query_sum
        + jnp.einsum("htk,khd->thd", text_dscore, text_key32, precision=HIGHEST_PRECISION) * factor
    )
    text_key_grad = (
        key_sum
        + jnp.einsum("htk,thd->khd", text_dscore, text_query32, precision=HIGHEST_PRECISION)
        * factor
    )
    text_value_grad = value_sum + jnp.einsum(
        "htk,thd->khd", text_prob, text_grad32, precision=HIGHEST_PRECISION
    )
    attended_rows = attended_blocks.reshape(token_rows, feature_width)
    query_grad_rows = query_grad_blocks.reshape(token_rows, feature_width)
    key_grad_rows = (
        own_key_grad.reshape(token_rows, feature_width)
        + video_key_from_text.reshape(token_rows, feature_width)
    ).astype(jnp.bfloat16)
    value_grad_rows = (
        own_value_grad.reshape(token_rows, feature_width)
        + video_value_from_text.reshape(token_rows, feature_width)
    ).astype(jnp.bfloat16)
    attended_video, video_query_grad, video_key_grad, video_value_grad = (
        lax.all_to_all(attended_rows, "head", split_axis=0, concat_axis=1, tiled=True),
        lax.all_to_all(query_grad_rows, "head", split_axis=0, concat_axis=1, tiled=True),
        lax.all_to_all(key_grad_rows, "head", split_axis=0, concat_axis=1, tiled=True),
        lax.all_to_all(value_grad_rows, "head", split_axis=0, concat_axis=1, tiled=True),
    )
    return (
        attended_video,
        video_query_grad,
        video_key_grad,
        video_value_grad,
        text_out.reshape(TXT, feature_width).astype(jnp.bfloat16),
        text_query_grad.reshape(TXT, feature_width).astype(jnp.bfloat16),
        text_key_grad.reshape(TXT, feature_width).astype(jnp.bfloat16),
        text_value_grad.reshape(TXT, feature_width).astype(jnp.bfloat16),
    )


def solution(mesh):
    placed = (
        P(("seq", "head"), None),
        P(("seq", "head"), None),
        P(("seq", "head"), None),
        P(("seq", "head"), None),
        P(None, "head"),
        P(None, "head"),
        P(None, "head"),
        P(None, "head"),
        P(),
        P(),
        P(),
    )
    return jax.shard_map(
        body,
        mesh=mesh,
        in_specs=placed,
        out_specs=(
            P(("seq", "head"), None),
            P(("seq", "head"), None),
            P(("seq", "head"), None),
            P(("seq", "head"), None),
            P(None, "head"),
            P(None, "head"),
            P(None, "head"),
            P(None, "head"),
        ),
        check_vma=False,
    )
```

profile of v0, /device:TPU:0, one launch (start us, length us, event | category | flops | bytes accessed | tf_op | source)
XLA Modules:
  0.0 900.4 jit_solution(9937720170638479781)
XLA Ops:
  50.8 66.3 %all-to-all-done.1 = bf16[8,256,768]{2,1,0:T(8,128)(2,1)} async-done(((bf16[8,256,768]{2,1,0:T(8,128)(2,1)}), bf16[8,256,768]{2,1,0:T(8,128)(2,1)}, u32[]{:S(2)}, u32[]{:S(2)}) %all-to-all-start.1) | async-done | bytes 3145760 | tf_op jit(solution)/shard_map/all_to_all | solution.py:183
  124.7 67.4 %all-to-all-done.3 = bf16[8,256,768]{2,1,0:T(8,128)(2,1)S(1)} async-done(((bf16[8,256,768]{2,1,0:T(8,128)(2,1)}), bf16[8,256,768]{2,1,0:T(8,128)(2,1)S(1)}, u32[]{:S(2)}, u32[]{:S(2)}) %all-to-all-start.3) | async-done | bytes 3145760 | tf_op jit(solution)/shard_map/all_to_all | solution.py:182
  212.1 13.7 %reshape.401 = bf16[4,1024,6,128]{3,2,1,0:T(8,128)(2,1)} reshape(bf16[32,128,768]{2,1,0:T(8,128)(2,1)} %gather_fusion.1) | data formatting | bytes 12582912 | tf_op jit(solution)/shard_map/while/body/eval_jaxpr/reshape | solution.py:175
  243.1 13.7 %reshape.400 = bf16[4,1024,6,128]{3,2,1,0:T(8,128)(2,1)} reshape(bf16[32,128,768]{2,1,0:T(8,128)(2,1)} %gather_fusion) | data formatting | bytes 12582912 | tf_op jit(solution)/shard_map/while/body/eval_jaxpr/reshape | solution.py:175
  256.8 11.5 %copy.380 = bf16[4,1024,6,128]{1,3,2,0:T(8,128)(2,1)} copy(bf16[4,1024,6,128]{3,2,1,0:T(8,128)(2,1)} %reshape.400) | data formatting | bytes 12582912 | tf_op jit(solution)/shard_map/while/body/eval_jaxpr/reshape | solution.py:175
  285.6 10.6 %bitcast_convert_fusion = (bf16[4,128,6,128]{1,3,2,0:T(8,128)(2,1)}, f32[4,6,128,128]{3,2,1,0:T(8,128)S(1)}) fusion(f32[4,6,1280,128]{3,2,1,0:T(8,128)} %copy-done.2, f32[4,6,128]{2,1,0:T(8,128)S(1)} %log_add_fusion, pred[4,1280]{1,0:T(4,128)(4,1)S(1)} %pad_add_fusion, bf16[4,256,6,128]{1,3,2,0:T(8,128)(2,1)S(1)} %broadcast_in_dim.182, ...), kind=kOutput, calls=%fused_computation.44 | convolution fusion | flops 1038483456 | bytes 25969664 | tf_op jit(solution)/shard_map/while/body/eval_jaxpr/bhtk,bkhd->bthd/dot_general | solution.py:36
  300.9 13.0 %fusion = bf16[4,6,128,1280]{2,3,1,0:T(8,128)(2,1)} fusion(f32[4,6,1280,128]{3,2,1,0:T(8,128)} %copy-done.2, bf16[4,128,6,128]{1,3,2,0:T(8,128)(2,1)S(1)} %bitcast.180, f32[4,6,128]{2,1,0:T(8,128)S(1)} %bitcast.208, f32[4,6,128]{2,1,0:T(8,128)S(1)} %log_add_fusion, pred[4,1280]{1,0:T(4,128)(4,1)S(1)} %pad_add_fusion, ...), kind=kOutput, calls=%fused_computation.9 | convolution fusion | flops 1045954560 | bytes 32273408 | tf_op jit(solution)/shard_map/while/body/eval_jaxpr/bthd,bkhd->bhtk/dot_general | solution.py:44
  326.8 11.1 %convolution_bitcast_fusion = f32[4,1280,6,128]{3,1,2,0:T(8,128)} fusion(bf16[4,128,6,128]{1,3,2,0:T(8,128)(2,1)S(1)} %bitcast.181, f32[4,6,1280,128]{3,2,1,0:T(8,128)} %copy-done.2, f32[4,6,128]{2,1,0:T(8,128)S(1)} %log_add_fusion, pred[4,1280]{1,0:T(4,128)(4,1)S(1)} %pad_add_fusion), kind=kOutput, calls=%fused_computation.19 | convolution fusion | flops 1022361600 | bytes 32261120 | tf_op jit(solution)/shard_map/while/body/eval_jaxpr/bhtk,bthd->bkhd/dot_general | solution.py:56
  337.9 10.4 %slice.43 = f32[4,1024,6,128]{3,1,2,0:T(8,128)} slice(f32[4,1280,6,128]{3,1,2,0:T(8,128)} %convolution_bitcast_fusion), slice={[0:4], [0:1024], [0:6], [0:128]} | slice | bytes 25165824 | tf_op jit(solution)/shard_map/while/body/eval_jaxpr/slice | solution.py:64
  348.3 17.8 %copy.498 = f32[4,1024,6,128]{3,2,1,0:T(8,128)} copy(f32[4,1024,6,128]{3,1,2,0:T(8,128)} %slice.43) | data formatting | bytes 25165824 | tf_op jit(solution)/shard_map/while/body/eval_jaxpr/reshape | solution.py:64
  366.1 16.1 %reshape.404 = f32[32,128,768]{2,1,0:T(8,128)} reshape(f32[4,1024,6,128]{3,2,1,0:T(8,128)} %copy.498) | data formatting | bytes 25165824 | tf_op jit(solution)/shard_map/while/body/eval_jaxpr/reshape | solution.py:64
  386.1 30.2 %scatter_fusion.2 = f32[20,128,768]{2,1,0:T(8,128)} fusion(f32[20,128,768]{2,1,0:T(8,128)} %broadcast.165.clone.1, s32[32]{0:T(128)S(1)} %reshape.345, f32[32,128,768]{2,1,0:T(8,128)} %reshape.404), kind=kCustom, calls=%fused_computation.4 | custom fusion | flops 3145728 | bytes 37748864 | tf_op jit(solution)/shard_map/while/body/eval_jaxpr/scatter-add | solution.py:66
  428.1 11.1 %multiply_bitcast_fusion = f32[4,1280,6,128]{3,1,2,0:T(8,128)} fusion(bf16[4,6,128,1280]{2,3,1,0:T(8,128)(2,1)} %fusion, bf16[4,128,6,128]{1,3,2,0:T(8,128)(2,1)} %bitcast.14), kind=kOutput, calls=%fused_computation.16 | convolution fusion | flops 1010565120 | bytes 24379392 | tf_op jit(solution)/shard_map/while/body/eval_jaxpr/bhtk,bthd->bkhd/dot_general | solution.py:53
  439.2 10.4 %slice.40 = f32[4,1024,6,128]{3,1,2,0:T(8,128)} slice(f32[4,1280,6,128]{3,1,2,0:T(8,128)} %multiply_bitcast_fusion), slice={[0:4], [0:1024], [0:6], [0:128]} | slice | bytes 25165824 | tf_op jit(solution)/shard_map/while/body/eval_jaxpr/slice | solution.py:64
  449.6 17.8 %copy.496 = f32[4,1024,6,128]{3,2,1,0:T(8,128)} copy(f32[4,1024,6,128]{3,1,2,0:T(8,128)} %slice.40) | data formatting | bytes 25165824 | tf_op jit(solution)/shard_map/while/body/eval_jaxpr/reshape | solution.py:64
  467.5 16.1 %reshape.402 = f32[32,128,768]{2,1,0:T(8,128)} reshape(f32[4,1024,6,128]{3,2,1,0:T(8,128)} %copy.496) | data formatting | bytes 25165824 | tf_op jit(solution)/shard_map/while/body/eval_jaxpr/reshape | solution.py:64
  487.5 30.1 %scatter_fusion = f32[20,128,768]{2,1,0:T(8,128)} fusion(f32[20,128,768]{2,1,0:T(8,128)} %broadcast.165.clone, s32[32]{0:T(128)S(1)} %reshape.345, f32[32,128,768]{2,1,0:T(8,128)} %reshape.402), kind=kCustom, calls=%fused_computation.2 | custom fusion | flops 3145728 | bytes 37748864 | tf_op jit(solution)/shard_map/while/body/eval_jaxpr/scatter-add | solution.py:66
  523.7 43.3 %all-to-all-done.10 = f32[8,256,768]{2,1,0:T(8,128)} async-done(((f32[8,256,768]{2,1,0:T(8,128)}), f32[8,256,768]{2,1,0:T(8,128)}, u32[]{:S(2)}, u32[]{:S(2)}) %all-to-all-start.10) | async-done | bytes 6291488 | tf_op jit(solution)/shard_map/all_to_all | solution.py:239
  583.2 103.5 %pmax.7 = f32[6,256]{1,0:T(8,128)} all-reduce(f32[6,256]{1,0:T(8,128)S(1)} %get-tuple-element.153), channel_id=1, replica_groups=mesh['seq'=8,'head'=4] {'seq'}, use_global_device_ids=true, to_apply=%region_12.13 | all-reduce | flops 1536 | bytes 12288 | tf_op jit(solution)/shard_map/pmax | solution.py:279
  692.2 44.9 %psum.35 = f32[6,256]{1,0:T(8,128)} all-reduce(f32[6,256]{1,0:T(8,128)S(1)} %fusion.9), channel_id=1, replica_groups=mesh['seq'=8,'head'=4] {'seq'}, use_global_device_ids=true, to_apply=%region_15.16 | all-reduce | flops 1536 | bytes 12288 | tf_op jit(solution)/shard_map/psum | solution.py:282
  747.5 32.2 %all-reduce.4.cloned.1.call-done = f32[256,6,128]{2,0,1:T(8,128)} async-done(((f32[256,6,128]{2,0,1:T(8,128)}), f32[256,6,128]{2,0,1:T(8,128)}) %all-reduce.4.cloned.1.call-update) | async-done | bytes 786448 | tf_op jit(solution)/shard_map/psum | solution.py:282
  812.2 9.2 %scatter_fusion.3 = f32[4,128,768]{2,1,0:T(8,128)S(1)} fusion(f32[4,128,768]{2,1,0:T(8,128)S(1)} %slice_add_fusion, s32[16]{0:T(128)S(1)} %copy-done.35, f32[16,128,768]{2,1,0:T(8,128)} %bitcast.47), kind=kCustom, calls=%fused_computation.5 | custom fusion | flops 1572864 | bytes 18874432 | tf_op jit(solution)/shard_map/scatter-add | solution.py:261
  833.5 29.9 %all-reduce.6.cloned.1.call-done = (f32[256,6,128]{2,0,1:T(8,128)}, f32[256,6,128]{2,0,1:T(8,128)}, f32[256,6,128]{0,2,1:T(8,128)}) async-done(((f32[256,6,128]{2,0,1:T(8,128)}, f32[256,6,128]{2,0,1:T(8,128)}, f32[256,6,128]{0,2,1:T(8,128)}), (f32[256,6,128]{2,0,1:T(8,128)}, f32[256,6,128]{2,0,1:T(8,128)}, f32[256,6,128]{0,2,1:T(8,128)})) %all-reduce.6.cloned.1.call-update) | async-done | bytes 2359312 | tf_op jit(solution)/shard_map/psum | solution.py:306
  868.4 9.2 %scatter_fusion.1 = f32[4,128,768]{2,1,0:T(8,128)S(1)} fusion(f32[4,128,768]{2,1,0:T(8,128)S(1)} %slice_add_fusion.1, s32[16]{0:T(128)S(1)} %copy-done.35, f32[16,128,768]{2,1,0:T(8,128)} %bitcast.41), kind=kCustom, calls=%fused_computation.3 | custom fusion | flops 1572864 | bytes 18874432 | tf_op jit(solution)/shard_map/scatter-add | solution.py:256
  (228 shorter events, 245.9 us)
Async XLA Ops:
  7.2 8.0 copy-start.33
  7.2 8.0 copy-start.38
  7.2 8.4 copy-start.26
  9.9 16.0 %all-to-all-start = ((bf16[128,4,768]{2,0,1:T(8,128)(2,1)}), bf16[128,4,768]{2,0,1:T(8,128)(2,1)S(1)}, u32[]{:S(2)}, u32[]{:S(2)}) async-start(bf16[128,4,768]{2,0,1:T(8,128)(2,1)} %copy.369), calls=%async_computation | async-start | bytes 1572864 | tf_op jit(solution)/shard_map/all_to_all | solution.py:90
  26.0 14.6 %all-to-all-start.2 = ((bf16[128,4,768]{2,0,1:T(8,128)(2,1)}), bf16[128,4,768]{2,0,1:T(8,128)(2,1)}, u32[]{:S(2)}, u32[]{:S(2)}) async-start(bf16[128,4,768]{2,0,1:T(8,128)(2,1)} %copy.382), calls=%async_computation.2 | async-start | bytes 1572864 | tf_op jit(solution)/shard_map/all_to_all | solution.py:89
  30.4 91.1 %copy-start.29 = (pred[8,8,2,4]{1,3,2,0:T(4,128)(4,1)}, pred[8,8,2,4]{1,3,2,0:T(4,128)(4,1)S(1)}, u32[]{:S(2)}) copy-start(pred[8,8,2,4]{1,3,2,0:T(4,128)(4,1)S(1)} %fusion.48) | copy-start | bytes 1540
  40.6 76.5 %all-to-all-start.1 = ((bf16[8,256,768]{2,1,0:T(8,128)(2,1)}), bf16[8,256,768]{2,1,0:T(8,128)(2,1)}, u32[]{:S(2)}, u32[]{:S(2)}) async-start(bf16[8,256,768]{2,1,0:T(8,128)(2,1)} %reshape.323), calls=%async_computation.1 | async-start | bytes 6291456 | tf_op jit(solution)/shard_map/all_to_all | solution.py:183
  50.8 70.0 %copy-start.39 = (s32[256]{0:T(256)S(1)}, s32[256]{0:T(256)}, u32[]{:S(2)}) copy-start(s32[256]{0:T(256)} %param.21) | copy-start | bytes 3076
  117.1 75.1 %all-to-all-start.3 = ((bf16[8,256,768]{2,1,0:T(8,128)(2,1)}), bf16[8,256,768]{2,1,0:T(8,128)(2,1)S(1)}, u32[]{:S(2)}, u32[]{:S(2)}) async-start(bf16[8,256,768]{2,1,0:T(8,128)(2,1)} %reshape.328), calls=%async_computation.3 | async-start | bytes 6291456 | tf_op jit(solution)/shard_map/all_to_all | solution.py:182
  192.2 76.1 %all-to-all-start.4 = ((bf16[128,4,768]{0,2,1:T(8,128)(2,1)}), bf16[128,4,768]{0,2,1:T(8,128)(2,1)}, u32[]{:S(2)}, u32[]{:S(2)}) async-start(bf16[128,4,768]{0,2,1:T(8,128)(2,1)} %bitcast.192), calls=%async_computation.4 | async-start | bytes 1572864 | tf_op jit(solution)/shard_map/all_to_all | solution.py:88
  197.8 8.5 copy-start.15
  225.7 7.5 copy-start.12
  256.8 15.7 %copy-start.25 = (bf16[256,6,128]{2,0,1:T(8,128)(2,1)S(1)}, bf16[256,6,128]{2,0,1:T(8,128)(2,1)}, u32[]{:S(2)}) copy-start(bf16[256,6,128]{2,0,1:T(8,128)(2,1)} %copy.385) | copy-start | bytes 1179652
  268.3 27.9 %all-to-all-start.6 = ((bf16[128,4,768]{0,2,1:T(8,128)(2,1)}), bf16[128,4,768]{0,2,1:T(8,128)(2,1)S(1)}, u32[]{:S(2)}, u32[]{:S(2)}) async-start(bf16[128,4,768]{0,2,1:T(8,128)(2,1)} %bitcast.20), calls=%async_computation.6 | async-start | bytes 1572864 | tf_op jit(solution)/shard_map/all_to_all | solution.py:91
  296.2 26.0 %all-to-all-start.5 = ((bf16[4,128,768]{1,2,0:T(8,128)(2,1)}), bf16[4,128,768]{1,2,0:T(8,128)(2,1)S(1)}, u32[]{:S(2)}, u32[]{:S(2)}) async-start(bf16[4,128,768]{1,2,0:T(8,128)(2,1)} %bitcast.203), calls=%async_computation.5 | async-start | bytes 1572864 | tf_op jit(solution)/shard_map/all_to_all | solution.py:330
  300.8 13.0 %copy-start.23 = (bf16[4,256,6,128]{3,1,2,0:T(8,128)(2,1)S(1)}, bf16[4,256,6,128]{3,1,2,0:T(8,128)(2,1)}, u32[]{:S(2)}) copy-start(bf16[4,256,6,128]{3,1,2,0:T(8,128)(2,1)} %copy-done.22) | copy-start | bytes 4718596
  322.2 15.7 %copy-start.20 = (bf16[4,128,768]{1,2,0:T(8,128)(2,1)}, bf16[4,128,768]{1,2,0:T(8,128)(2,1)S(1)}, u32[]{:S(2)}) copy-start(bf16[4,128,768]{1,2,0:T(8,128)(2,1)S(1)} %all-to-all-done.5) | copy-start | bytes 2359300
  322.2 100.2 %all-to-all-start.7 = ((bf16[4,128,768]{1,2,0:T(8,128)(2,1)}), bf16[4,128,768]{1,2,0:T(8,128)(2,1)S(1)}, u32[]{:S(2)}, u32[]{:S(2)}) async-start(bf16[4,128,768]{1,2,0:T(8,128)(2,1)} %bitcast.202), calls=%async_computation.7 | async-start | bytes 1572864 | tf_op jit(solution)/shard_map/all_to_all | solution.py:331
  423.4 143.7 %all-to-all-start.10 = ((f32[8,256,768]{2,1,0:T(8,128)}), f32[8,256,768]{2,1,0:T(8,128)}, u32[]{:S(2)}, u32[]{:S(2)}) async-start(f32[8,256,768]{2,1,0:T(8,128)} %bitcast.163), calls=%async_computation.10 | async-start | bytes 12582912 | tf_op jit(solution)/shard_map/all_to_all | solution.py:239
  567.1 255.4 %all-to-all-start.8 = ((f32[8,256,768]{2,1,0:T(8,128)}), f32[8,256,768]{2,1,0:T(8,128)}, u32[]{:S(2)}, u32[]{:S(2)}) async-start(f32[8,256,768]{2,1,0:T(8,128)} %bitcast.162), calls=%async_computation.8 | async-start | bytes 12582912 | tf_op jit(solution)/shard_map/all_to_all | solution.py:232
  572.0 207.6 %all-reduce.4.cloned.1.call-start = ((), (), s32[]{:S(2)}) async-start(), calls=%async_computation.12 | async-start | bytes 1572864 | tf_op jit(solution)/shard_map/psum | solution.py:282
  691.2 172.3 %all-reduce.6.cloned.1.call-start = ((), (), s32[]{:S(2)}) async-start(), calls=%async_computation.13 | async-start | bytes 4718592 | tf_op jit(solution)/shard_map/psum | solution.py:306
  822.4 56.1 %all-to-all-start.11 = ((bf16[4,128,768]{2,1,0:T(8,128)(2,1)}), bf16[4,128,768]{2,1,0:T(8,128)(2,1)}, u32[]{:S(2)}, u32[]{:S(2)}) async-start(bf16[4,128,768]{2,1,0:T(8,128)(2,1)} %convert_element_type.127), calls=%async_computation.11 | async-start | bytes 1572864 | tf_op jit(solution)/shard_map/all_to_all | solution.py:333
  878.5 13.3 %all-to-all-start.9 = ((bf16[4,128,768]{2,1,0:T(8,128)(2,1)}), bf16[4,128,768]{2,1,0:T(8,128)(2,1)S(1)}, u32[]{:S(2)}, u32[]{:S(2)}) async-start(bf16[4,128,768]{2,1,0:T(8,128)(2,1)} %convert_element_type.123), calls=%async_computation.9 | async-start | bytes 1572864 | tf_op jit(solution)/shard_map/all_to_all | solution.py:332
  (30 other events, 130.1 us)
Sparse Core Ops, SparseCore 0:
  691.3 88.3 all-reduce.3
  797.1 66.2 all-reduce.5
where the time goes:
time: 911 us; the launch traced here: 900 us
  waiting for transfers between devices  253 us (28%)
  local copies, waits for them, and re-layouts  228 us (25%)
  blocking collectives  148 us (16%)
  other arithmetic  109 us (12%)
  matrix products  94.3 us (10%)
  starting transfers between devices  53.4 us (6%)
  between operations  14.9 us (2%)
    pmax x1, blocking collectives, body(): lax.pmax(jnp.max(video_scores, axis=-1), 'seq')  104 us
    reshape x4, local copies, waits for them, and re-layouts, spread_grads(): grad_blk[:, :KT * TILE].reshape(block_tiles, KT, TILE, pool_total.shape[2])  67.9 us
    all_to_all x1, waiting for transfers between devices, body(): lax.all_to_all(send_keys, 'seq', split_axis=0, concat_axis=0, tiled=True)  67.4 us
    all_to_all x1, waiting for transfers between devices, body(): lax.all_to_all(send_values, 'seq', split_axis=0, concat_axis=0, tiled=True)  66.3 us
    scatter-add x2, other arithmetic, spread_grads(): pool_total.at[pool_slot].add(tile_part)  60.3 us
    reshape x4, local copies, waits for them, and re-layouts, block_rows(): picked = pool[slot_blk].reshape(block_tiles, KT * TILE, head_count, HD)  46.3 us
    psum x1, blocking collectives, body(): lax.psum((jnp.sum(video_exp, axis=-1), split_product('htk,khd->thd', vide...  44.9 us
    all_to_all x1, waiting for transfers between devices, body(): lax.all_to_all(value_acc[shard_tiles:].reshape(groups, MOST * TILE, featu...  43.3 us
  transfers between devices with their start and end apart: 14, of which 8 were waited for; matrix products, arithmetic and copies ran while one was open for 47% of the time, Pallas kernels for 0%

commit v1 on v0

--- a/solution.py
+++ b/solution.py
@@ -2,6 +2,7 @@
 import jax.numpy as jnp
 from jax import lax
 from jax.sharding import PartitionSpec as P
+from jax.lax import axis_index, axis_size, ppermute
 
 HD = 128
 TXT = 256
@@ -10,6 +11,24 @@
 MOST = 2
 NEGATIVE = -1e30
 HIGHEST_PRECISION = lax.Precision.HIGHEST
+
+
+def form_group(load):
+    axis_id = "seq"
+    seen_now = axis_size(axis_id)
+    value_now, ready = (seen_now, axis_index(axis_id))
+    oldest = load.shape[0] // value_now
+    big = jnp.roll(load, shift=-ready * oldest, axis=0)
+    buffer = [lax.slice_in_dim(big, 0, oldest, axis=0)]
+    for idx in range(1, value_now):
+        back = lax.slice_in_dim(big, idx * oldest, (idx + 1) * oldest, axis=0)
+        s_next = ppermute(
+            back, axis_id, perm=[(w, (w + idx) % value_now) for w in range(value_now)]
+        )
+        buffer.append(s_next)
+    local_next = jnp.concatenate(buffer[::-1], axis=0)
+    z1 = jnp.roll(local_next, (ready + 1) * buffer[0].shape[0], axis=0)
+    return z1
 
 
 def split_product(form, weights, data):
@@ -180,7 +199,7 @@
     pool_keys, pool_values = build_pool(
         (
             lax.all_to_all(send_keys, "seq", split_axis=0, concat_axis=0, tiled=True),
-            lax.all_to_all(send_values, "seq", split_axis=0, concat_axis=0, tiled=True),
+            form_group(send_values),
         )
     )
     start = (

time: 911 us -> 1020 us (1.12)
  starting transfers between devices: 53.4 us -> 129 us
  local copies, waits for them, and re-layouts: 228 us -> 268 us
  waiting for transfers between devices: 253 us -> 225 us
    ppermute x0 -> x7, starting transfers between devices: none -> 76 us  [form_group(): ppermute(back, axis_id, perm=[(w, (w + idx) % value_now) for w in range(v...]
    all_to_all x1, waiting for transfers between devices: 67.4 us -> 0.01 us  [body(): lax.all_to_all(send_keys, 'seq', split_axis=0, concat_axis=0, tiled=True)]
    ppermute x0 -> x7, waiting for transfers between devices: none -> 44.4 us  [form_group(): ppermute(back, axis_id, perm=[(w, (w + idx) % value_now) for w in range(v...]
    reshape x4 -> x6, local copies, waits for them, and re-layouts: 46.3 us -> 67.5 us  [block_rows(): picked = pool[slot_blk].reshape(block_tiles, KT * TILE, head_count, HD)]
    unnamed x98 -> x116, local copies, waits for them, and re-layouts: 23.1 us -> 28.3 us
  transfers between devices with their start and end apart: 14 -> 21, of which waited for: 8 -> 9; matrix products, arithmetic and copies ran while one was open for 47% -> 47% of each run, Pallas kernels for 0% -> 0%
where the time goes in v1:
time: 1020 us; the launch traced here: 1010 us
  local copies, waits for them, and re-layouts  268 us (26%)
  waiting for transfers between devices  225 us (22%)
  blocking collectives  149 us (15%)
  starting transfers between devices  129 us (13%)
  other arithmetic  119 us (12%)
  matrix products  100 us (10%)
  between operations  15 us (1%)
    pmax x1, blocking collectives, body(): lax.pmax(jnp.max(video_scores, axis=-1), 'seq')  104 us
    ppermute x7, starting transfers between devices, form_group(): ppermute(back, axis_id, perm=[(w, (w + idx) % value_now) for w in range(v...  76 us
    reshape x4, local copies, waits for them, and re-layouts, spread_grads(): grad_blk[:, :KT * TILE].reshape(block_tiles, KT, TILE, pool_total.shape[2])  67.9 us
    reshape x6, local copies, waits for them, and re-layouts, block_rows(): picked = pool[slot_blk].reshape(block_tiles, KT * TILE, head_count, HD)  67.5 us
    all_to_all x1, waiting for transfers between devices, body(): lax.all_to_all(send_values, 'seq', split_axis=0, concat_axis=0, tiled=True)  64.4 us
    scatter-add x2, other arithmetic, spread_grads(): pool_total.at[pool_slot].add(tile_part)  60.4 us
    psum x1, blocking collectives, body(): lax.psum((jnp.sum(video_exp, axis=-1), split_product('htk,khd->thd', vide...  44.8 us
    ppermute x7, waiting for transfers between devices, form_group(): ppermute(back, axis_id, perm=[(w, (w + idx) % value_now) for w in range(v...  44.4 us
  transfers between devices with their start and end apart: 21, of which 9 were waited for; matrix products, arithmetic and copies ran while one was open for 47% of the time, Pallas kernels for 0%

profile of v1, /device:TPU:0, one launch (start us, length us, event | category | flops | bytes accessed | tf_op | source)
XLA Modules:
  0.0 1005.4 jit_solution(2588712281314268306)
XLA Ops:
  51.9 64.4 %all-to-all-done.5 = bf16[8,256,768]{2,1,0:T(8,128)(2,1)} async-done(((bf16[8,256,768]{2,1,0:T(8,128)(2,1)}), bf16[8,256,768]{2,1,0:T(8,128)(2,1)}, u32[]{:S(2)}, u32[]{:S(2)}) %all-to-all-start.5) | async-done | bytes 3145760 | tf_op jit(solution)/shard_map/all_to_all | solution.py:227
  140.5 40.7 %collective-permute-done = bf16[1,256,768]{2,1,0:T(8,128)(2,1)} collective-permute-done((bf16[1,256,768]{2,1,0:T(8,128)(2,1)}, bf16[1,256,768]{2,1,0:T(8,128)(2,1)}, u32[]{:S(2)}, u32[]{:S(2)}) %collective-permute-start) | collective-permute-done | bytes 393248 | tf_op jit(solution)/shard_map/ppermute | solution.py:25
  181.1 45.4 %collective-permute-start.4 = (bf16[1,256,768]{2,1,0:T(8,128)(2,1)}, bf16[1,256,768]{2,1,0:T(8,128)(2,1)S(1)}, u32[]{:S(2)}, u32[]{:S(2)}) collective-permute-start(bf16[1,256,768]{2,1,0:T(8,128)(2,1)} %get-tuple-element.148), channel_id=1, source_target_pairs={{0,12},{4,16},{8,20},{12,24},{16,28},{20,0},{24,4},{28,8},{1,13},{... | collective-permute-start | bytes 1179656 | tf_op jit(solution)/shard_map/ppermute | solution.py:25
  228.3 24.0 %collective-permute-start.5 = (bf16[1,256,768]{2,1,0:T(8,128)(2,1)}, bf16[1,256,768]{2,1,0:T(8,128)(2,1)S(1)}, u32[]{:S(2)}, u32[]{:S(2)}) collective-permute-start(bf16[1,256,768]{2,1,0:T(8,128)(2,1)} %get-tuple-element.147), channel_id=1, source_target_pairs={{0,8},{4,12},{8,16},{12,20},{16,24},{20,28},{24,0},{28,4},{1,9},{5... | collective-permute-start | bytes 1179656 | tf_op jit(solution)/shard_map/ppermute | solution.py:25
  283.8 13.7 %reshape.417 = bf16[4,1024,6,128]{3,2,1,0:T(8,128)(2,1)} reshape(bf16[32,128,768]{2,1,0:T(8,128)(2,1)} %gather_fusion.1) | data formatting | bytes 12582912 | tf_op jit(solution)/shard_map/while/body/eval_jaxpr/reshape | solution.py:194
  315.7 13.7 %reshape.416 = bf16[4,1024,6,128]{3,2,1,0:T(8,128)(2,1)} reshape(bf16[32,128,768]{2,1,0:T(8,128)(2,1)} %gather_fusion) | data formatting | bytes 12582912 | tf_op jit(solution)/shard_map/while/body/eval_jaxpr/reshape | solution.py:194
  329.3 11.5 %copy.389 = bf16[4,1024,6,128]{1,3,2,0:T(8,128)(2,1)} copy(bf16[4,1024,6,128]{3,2,1,0:T(8,128)(2,1)} %reshape.416) | data formatting | bytes 12582912 | tf_op jit(solution)/shard_map/while/body/eval_jaxpr/reshape | solution.py:194
  360.8 10.9 %bitcast_convert_fusion = (bf16[4,128,6,128]{1,3,2,0:T(8,128)(2,1)}, f32[4,6,128,128]{3,2,1,0:T(8,128)}) fusion(f32[4,6,1280,128]{3,2,1,0:T(8,128)} %copy-done.2, f32[4,6,128]{2,1,0:T(8,128)S(1)} %log_add_fusion, pred[4,1280]{1,0:T(4,128)(4,1)S(1)} %pad_add_fusion, bf16[4,256,6,128]{1,3,2,0:T(8,128)(2,1)S(1)} %broadcast_in_dim.182, ...), kind=kOutput, calls=%fused_computation.57 | convolution fusion | flops 1038483456 | bytes 25969664 | tf_op jit(solution)/shard_map/while/body/eval_jaxpr/bhtk,bkhd->bthd/dot_general | solution.py:55
  377.4 13.7 %reshape.418 = bf16[4,1024,6,128]{3,2,1,0:T(8,128)(2,1)} reshape(bf16[32,128,768]{2,1,0:T(8,128)(2,1)} %gather_fusion.2) | data formatting | bytes 12582912 | tf_op jit(solution)/shard_map/while/body/eval_jaxpr/reshape | solution.py:194
  406.0 12.2 %fusion = bf16[4,6,128,1280]{2,3,1,0:T(8,128)(2,1)} fusion(f32[4,6,1280,128]{3,2,1,0:T(8,128)} %copy-done.2, bf16[4,128,6,128]{1,3,2,0:T(8,128)(2,1)S(1)} %bitcast.186, bf16[4,256,6,128]{3,1,2,0:T(8,128)(2,1)} %broadcast_in_dim.182.clone, bf16[4,1024,6,128]{3,1,2,0:T(8,128)(2,1)} %copy.401, f32[4,6,128]{2,1,0:T(8,128)S(1)} %bitcast.216, ...), kind=kOutput, calls=%fused_computation.10 | convolution fusion | flops 1045954560 | bytes 32273408 | tf_op jit(solution)/shard_map/while/body/eval_jaxpr/bthd,bkhd->bhtk/dot_general | solution.py:63
  431.8 11.1 %convolution_bitcast_fusion = f32[4,1280,6,128]{3,1,2,0:T(8,128)} fusion(bf16[4,128,6,128]{1,3,2,0:T(8,128)(2,1)S(1)} %bitcast.187, f32[4,6,1280,128]{3,2,1,0:T(8,128)} %copy-done.2, f32[4,6,128]{2,1,0:T(8,128)S(1)} %copy-done.35, pred[4,1280]{1,0:T(4,128)(4,1)S(1)} %pad_add_fusion), kind=kOutput, calls=%fused_computation.20 | convolution fusion | flops 1022361600 | bytes 32261120 | tf_op jit(solution)/shard_map/while/body/eval_jaxpr/bhtk,bthd->bkhd/dot_general | solution.py:75
  453.2 17.9 %copy.510 = f32[4,1024,6,128]{3,2,1,0:T(8,128)} copy(f32[4,1024,6,128]{3,1,2,0:T(8,128)} %slice.85) | data formatting | bytes 25165824 | tf_op jit(solution)/shard_map/while/body/eval_jaxpr/reshape | solution.py:83
  471.0 16.0 %reshape.421 = f32[32,128,768]{2,1,0:T(8,128)} reshape(f32[4,1024,6,128]{3,2,1,0:T(8,128)} %copy.510) | data formatting | bytes 25165824 | tf_op jit(solution)/shard_map/while/body/eval_jaxpr/reshape | solution.py:83
  491.0 30.3 %scatter_fusion.2 = f32[20,128,768]{2,1,0:T(8,128)} fusion(f32[20,128,768]{2,1,0:T(8,128)} %broadcast.166.clone.1, s32[32]{0:T(128)S(1)} %reshape.351, f32[32,128,768]{2,1,0:T(8,128)} %reshape.421), kind=kCustom, calls=%fused_computation.5 | custom fusion | flops 3145728 | bytes 37748864 | tf_op jit(solution)/shard_map/while/body/eval_jaxpr/scatter-add | solution.py:85
  533.1 11.0 %multiply_bitcast_fusion = f32[4,1280,6,128]{3,1,2,0:T(8,128)} fusion(bf16[4,6,128,1280]{2,3,1,0:T(8,128)(2,1)} %fusion, bf16[4,128,6,128]{1,3,2,0:T(8,128)(2,1)S(1)} %bitcast.196), kind=kOutput, calls=%fused_computation.17 | convolution fusion | flops 1010565120 | bytes 24379392 | tf_op jit(solution)/shard_map/while/body/eval_jaxpr/bhtk,bthd->bkhd/dot_general | solution.py:72
  544.1 10.4 %slice.82 = f32[4,1024,6,128]{3,1,2,0:T(8,128)} slice(f32[4,1280,6,128]{3,1,2,0:T(8,128)} %multiply_bitcast_fusion), slice={[0:4], [0:1024], [0:6], [0:128]} | slice | bytes 25165824 | tf_op jit(solution)/shard_map/while/body/eval_jaxpr/slice | solution.py:83
  554.5 17.9 %copy.508 = f32[4,1024,6,128]{3,2,1,0:T(8,128)} copy(f32[4,1024,6,128]{3,1,2,0:T(8,128)} %slice.82) | data formatting | bytes 25165824 | tf_op jit(solution)/shard_map/while/body/eval_jaxpr/reshape | solution.py:83
  572.3 16.1 %reshape.419 = f32[32,128,768]{2,1,0:T(8,128)} reshape(f32[4,1024,6,128]{3,2,1,0:T(8,128)} %copy.508) | data formatting | bytes 25165824 | tf_op jit(solution)/shard_map/while/body/eval_jaxpr/reshape | solution.py:83
  592.4 30.1 %scatter_fusion = f32[20,128,768]{2,1,0:T(8,128)} fusion(f32[20,128,768]{2,1,0:T(8,128)} %broadcast.166.clone, s32[32]{0:T(128)S(1)} %reshape.351, f32[32,128,768]{2,1,0:T(8,128)} %reshape.419), kind=kCustom, calls=%fused_computation.3 | custom fusion | flops 3145728 | bytes 37748864 | tf_op jit(solution)/shard_map/while/body/eval_jaxpr/scatter-add | solution.py:85
  628.6 43.4 %all-to-all-done.10 = f32[8,256,768]{2,1,0:T(8,128)} async-done(((f32[8,256,768]{2,1,0:T(8,128)}), f32[8,256,768]{2,1,0:T(8,128)}, u32[]{:S(2)}, u32[]{:S(2)}) %all-to-all-start.10) | async-done | bytes 6291488 | tf_op jit(solution)/shard_map/all_to_all | solution.py:258
  687.3 104.4 %pmax.7 = f32[6,256]{1,0:T(8,128)} all-reduce(f32[6,256]{1,0:T(8,128)S(1)} %get-tuple-element.163), channel_id=1, replica_groups=mesh['seq'=8,'head'=4] {'seq'}, use_global_device_ids=true, to_apply=%region_12.14 | all-reduce | flops 1536 | bytes 12288 | tf_op jit(solution)/shard_map/pmax | solution.py:298
  797.2 44.8 %psum.35 = f32[6,256]{1,0:T(8,128)} all-reduce(f32[6,256]{1,0:T(8,128)S(1)} %fusion.17), channel_id=1, replica_groups=mesh['seq'=8,'head'=4] {'seq'}, use_global_device_ids=true, to_apply=%region_15.17 | all-reduce | flops 1536 | bytes 12288 | tf_op jit(solution)/shard_map/psum | solution.py:301
  852.4 32.2 %all-reduce.4.cloned.1.call-done = f32[256,6,128]{2,0,1:T(8,128)} async-done(((f32[256,6,128]{2,0,1:T(8,128)}), f32[256,6,128]{2,0,1:T(8,128)}) %all-reduce.4.cloned.1.call-update) | async-done | bytes 786448 | tf_op jit(solution)/shard_map/psum | solution.py:301
  938.6 29.8 %all-reduce.6.cloned.1.call-done = (f32[256,6,128]{2,0,1:T(8,128)}, f32[256,6,128]{2,0,1:T(8,128)}, f32[256,6,128]{0,2,1:T(8,128)}) async-done(((f32[256,6,128]{2,0,1:T(8,128)}, f32[256,6,128]{2,0,1:T(8,128)}, f32[256,6,128]{0,2,1:T(8,128)}), (f32[256,6,128]{2,0,1:T(8,128)}, f32[256,6,128]{2,0,1:T(8,128)}, f32[256,6,128]{0,2,1:T(8,128)})) %all-reduce.6.cloned.1.call-update) | async-done | bytes 2359312 | tf_op jit(solution)/shard_map/psum | solution.py:325
  (268 shorter events, 324.8 us)
Async XLA Ops:
  9.9 16.0 %all-to-all-start = ((bf16[128,4,768]{2,0,1:T(8,128)(2,1)}), bf16[128,4,768]{2,0,1:T(8,128)(2,1)S(1)}, u32[]{:S(2)}, u32[]{:S(2)}) async-start(bf16[128,4,768]{2,0,1:T(8,128)(2,1)} %copy.378), calls=%async_computation | async-start | bytes 1572864 | tf_op jit(solution)/shard_map/all_to_all | solution.py:109
  26.0 279.1 %copy-start.8 = (bf16[128,4,768]{2,0,1:T(8,128)(2,1)}, bf16[128,4,768]{2,0,1:T(8,128)(2,1)S(1)}, u32[]{:S(2)}) copy-start(bf16[128,4,768]{2,0,1:T(8,128)(2,1)S(1)} %all-to-all-done) | copy-start | bytes 2359300
  26.0 13.8 %all-to-all-start.1 = ((bf16[128,4,768]{2,0,1:T(8,128)(2,1)}), bf16[128,4,768]{2,0,1:T(8,128)(2,1)S(1)}, u32[]{:S(2)}, u32[]{:S(2)}) async-start(bf16[128,4,768]{2,0,1:T(8,128)(2,1)} %copy.391), calls=%async_computation.1 | async-start | bytes 1572864 | tf_op jit(solution)/shard_map/all_to_all | solution.py:108
  39.8 234.2 %copy-start.15 = (bf16[128,4,768]{2,0,1:T(8,128)(2,1)}, bf16[128,4,768]{2,0,1:T(8,128)(2,1)S(1)}, u32[]{:S(2)}) copy-start(bf16[128,4,768]{2,0,1:T(8,128)(2,1)S(1)} %all-to-all-done.1) | copy-start | bytes 2359300
  39.8 76.5 %all-to-all-start.5 = ((bf16[8,256,768]{2,1,0:T(8,128)(2,1)}), bf16[8,256,768]{2,1,0:T(8,128)(2,1)}, u32[]{:S(2)}, u32[]{:S(2)}) async-start(bf16[8,256,768]{2,1,0:T(8,128)(2,1)} %reshape.327), calls=%async_computation.5 | async-start | bytes 6291456 | tf_op jit(solution)/shard_map/all_to_all | solution.py:227
  116.3 149.3 %all-to-all-start.2 = ((bf16[8,256,768]{2,1,0:T(8,128)(2,1)}), bf16[8,256,768]{2,1,0:T(8,128)(2,1)}, u32[]{:S(2)}, u32[]{:S(2)}) async-start(bf16[8,256,768]{2,1,0:T(8,128)(2,1)} %reshape.332), calls=%async_computation.2 | async-start | bytes 6291456 | tf_op jit(solution)/shard_map/all_to_all | solution.py:201
  128.6 52.5 %collective-permute-start = (bf16[1,256,768]{2,1,0:T(8,128)(2,1)}, bf16[1,256,768]{2,1,0:T(8,128)(2,1)}, u32[]{:S(2)}, u32[]{:S(2)}) collective-permute-start(bf16[1,256,768]{2,1,0:T(8,128)(2,1)} %get-tuple-element.152), channel_id=1, source_target_pairs={{0,28},{4,0},{8,4},{12,8},{16,12},{20,16},{24,20},{28,24},{1,29},{... | collective-permute-start | bytes 1179656 | tf_op jit(solution)/shard_map/ppermute | solution.py:25
  132.3 121.8 %collective-permute-start.2 = (bf16[1,256,768]{2,1,0:T(8,128)(2,1)}, bf16[1,256,768]{2,1,0:T(8,128)(2,1)}, u32[]{:S(2)}, u32[]{:S(2)}) collective-permute-start(bf16[1,256,768]{2,1,0:T(8,128)(2,1)} %get-tuple-element.150), channel_id=1, source_target_pairs={{0,20},{4,24},{8,28},{12,0},{16,4},{20,8},{24,12},{28,16},{1,21},{... | collective-permute-start | bytes 1179656 | tf_op jit(solution)/shard_map/ppermute | solution.py:25
  132.4 96.0 %collective-permute-start.1 = (bf16[1,256,768]{2,1,0:T(8,128)(2,1)}, bf16[1,256,768]{2,1,0:T(8,128)(2,1)}, u32[]{:S(2)}, u32[]{:S(2)}) collective-permute-start(bf16[1,256,768]{2,1,0:T(8,128)(2,1)} %get-tuple-element.151), channel_id=1, source_target_pairs={{0,24},{4,28},{8,0},{12,4},{16,8},{20,12},{24,16},{28,20},{1,25},{... | collective-permute-start | bytes 1179656 | tf_op jit(solution)/shard_map/ppermute | solution.py:25
  133.3 126.4 %collective-permute-start.3 = (bf16[1,256,768]{2,1,0:T(8,128)(2,1)}, bf16[1,256,768]{2,1,0:T(8,128)(2,1)}, u32[]{:S(2)}, u32[]{:S(2)}) collective-permute-start(bf16[1,256,768]{2,1,0:T(8,128)(2,1)} %get-tuple-element.149), channel_id=1, source_target_pairs={{0,16},{4,20},{8,24},{12,28},{16,0},{20,4},{24,8},{28,12},{1,17},{... | collective-permute-start | bytes 1179656 | tf_op jit(solution)/shard_map/ppermute | solution.py:25
  136.1 224.5 %copy-start.21 = (bf16[256,768]{0,1:T(8,128)(2,1)}, bf16[256,768]{0,1:T(8,128)(2,1)S(1)}, u32[]{:S(2)}) copy-start(bf16[256,768]{0,1:T(8,128)(2,1)S(1)} %copy.388) | copy-start | bytes 1179652
  139.8 123.2 %collective-permute-start.6 = (bf16[1,256,768]{2,1,0:T(8,128)(2,1)}, bf16[1,256,768]{2,1,0:T(8,128)(2,1)S(1)}, u32[]{:S(2)}, u32[]{:S(2)}) collective-permute-start(bf16[1,256,768]{2,1,0:T(8,128)(2,1)} %get-tuple-element.146), channel_id=1, source_target_pairs={{0,4},{4,8},{8,12},{12,16},{16,20},{20,24},{24,28},{28,0},{1,5},{5... | collective-permute-start | bytes 1179656 | tf_op jit(solution)/shard_map/ppermute | solution.py:25
  181.1 80.3 %collective-permute-start.4 = (bf16[1,256,768]{2,1,0:T(8,128)(2,1)}, bf16[1,256,768]{2,1,0:T(8,128)(2,1)S(1)}, u32[]{:S(2)}, u32[]{:S(2)}) collective-permute-start(bf16[1,256,768]{2,1,0:T(8,128)(2,1)} %get-tuple-element.148), channel_id=1, source_target_pairs={{0,12},{4,16},{8,20},{12,24},{16,28},{20,0},{24,4},{28,8},{1,13},{... | collective-permute-start | bytes 1179656 | tf_op jit(solution)/shard_map/ppermute | solution.py:25
  228.3 33.9 %collective-permute-start.5 = (bf16[1,256,768]{2,1,0:T(8,128)(2,1)}, bf16[1,256,768]{2,1,0:T(8,128)(2,1)S(1)}, u32[]{:S(2)}, u32[]{:S(2)}) collective-permute-start(bf16[1,256,768]{2,1,0:T(8,128)(2,1)} %get-tuple-element.147), channel_id=1, source_target_pairs={{0,8},{4,12},{8,16},{12,20},{16,24},{20,28},{24,0},{28,4},{1,9},{5... | collective-permute-start | bytes 1179656 | tf_op jit(solution)/shard_map/ppermute | solution.py:25
  265.6 75.2 %all-to-all-start.3 = ((bf16[128,4,768]{0,2,1:T(8,128)(2,1)}), bf16[128,4,768]{0,2,1:T(8,128)(2,1)S(1)}, u32[]{:S(2)}, u32[]{:S(2)}) async-start(bf16[128,4,768]{0,2,1:T(8,128)(2,1)} %bitcast.201), calls=%async_computation.3 | async-start | bytes 1572864 | tf_op jit(solution)/shard_map/all_to_all | solution.py:107
  340.8 57.6 %all-to-all-start.6 = ((bf16[128,4,768]{0,2,1:T(8,128)(2,1)}), bf16[128,4,768]{0,2,1:T(8,128)(2,1)S(1)}, u32[]{:S(2)}, u32[]{:S(2)}) async-start(bf16[128,4,768]{0,2,1:T(8,128)(2,1)} %bitcast.21), calls=%async_computation.6 | async-start | bytes 1572864 | tf_op jit(solution)/shard_map/all_to_all | solution.py:110
  398.4 28.7 %all-to-all-start.4 = ((bf16[4,128,768]{1,2,0:T(8,128)(2,1)}), bf16[4,128,768]{1,2,0:T(8,128)(2,1)S(1)}, u32[]{:S(2)}, u32[]{:S(2)}) async-start(bf16[4,128,768]{1,2,0:T(8,128)(2,1)} %bitcast.17), calls=%async_computation.4 | async-start | bytes 1572864 | tf_op jit(solution)/shard_map/all_to_all | solution.py:349
  427.1 100.3 %all-to-all-start.7 = ((bf16[4,128,768]{1,2,0:T(8,128)(2,1)}), bf16[4,128,768]{1,2,0:T(8,128)(2,1)S(1)}, u32[]{:S(2)}, u32[]{:S(2)}) async-start(bf16[4,128,768]{1,2,0:T(8,128)(2,1)} %bitcast.211), calls=%async_computation.7 | async-start | bytes 1572864 | tf_op jit(solution)/shard_map/all_to_all | solution.py:350
  528.3 143.7 %all-to-all-start.10 = ((f32[8,256,768]{2,1,0:T(8,128)}), f32[8,256,768]{2,1,0:T(8,128)}, u32[]{:S(2)}, u32[]{:S(2)}) async-start(f32[8,256,768]{2,1,0:T(8,128)} %bitcast.166), calls=%async_computation.10 | async-start | bytes 12582912 | tf_op jit(solution)/shard_map/all_to_all | solution.py:258
  672.1 255.4 %all-to-all-start.8 = ((f32[8,256,768]{2,1,0:T(8,128)}), f32[8,256,768]{2,1,0:T(8,128)}, u32[]{:S(2)}, u32[]{:S(2)}) async-start(f32[8,256,768]{2,1,0:T(8,128)} %bitcast.165), calls=%async_computation.8 | async-start | bytes 12582912 | tf_op jit(solution)/shard_map/all_to_all | solution.py:251
  677.1 207.6 %all-reduce.4.cloned.1.call-start = ((), (), s32[]{:S(2)}) async-start(), calls=%async_computation.12 | async-start | bytes 1572864 | tf_op jit(solution)/shard_map/psum | solution.py:301
  796.2 172.2 %all-reduce.6.cloned.1.call-start = ((), (), s32[]{:S(2)}) async-start(), calls=%async_computation.13 | async-start | bytes 4718592 | tf_op jit(solution)/shard_map/psum | solution.py:325
  927.5 56.0 %all-to-all-start.11 = ((bf16[4,128,768]{2,1,0:T(8,128)(2,1)}), bf16[4,128,768]{2,1,0:T(8,128)(2,1)}, u32[]{:S(2)}, u32[]{:S(2)}) async-start(bf16[4,128,768]{2,1,0:T(8,128)(2,1)} %convert_element_type.127), calls=%async_computation.11 | async-start | bytes 1572864 | tf_op jit(solution)/shard_map/all_to_all | solution.py:352
  983.5 13.3 %all-to-all-start.9 = ((bf16[4,128,768]{2,1,0:T(8,128)(2,1)}), bf16[4,128,768]{2,1,0:T(8,128)(2,1)S(1)}, u32[]{:S(2)}, u32[]{:S(2)}) async-start(bf16[4,128,768]{2,1,0:T(8,128)(2,1)} %convert_element_type.123), calls=%async_computation.9 | async-start | bytes 1572864 | tf_op jit(solution)/shard_map/all_to_all | solution.py:351
  (42 other events, 519.2 us)
Sparse Core Ops, SparseCore 0:
  796.3 88.3 all-reduce.3
  902.2 66.1 all-reduce.5
